TPU v7x, 512 devices: a whole 4x4x16 slice. The times are simulated.
512 devices in a mesh: gx: 64 (over z_lo, x, core), yz: 8 (over y, z_hi).
Axes of the slice: x: 4, y: 4, z: 16 (z_hi: 2, z_lo: 8; z = z_hi * 8 + z_lo), core: 2. Of those that a mesh axis runs over, the one named last changes fastest.
Arguments:
- solution: float32 [4, 512, 64, 3, 128], P(None, 'gx', 'yz'), may hold values from -6 to 6
- residual: float32 [4, 512, 64, 3, 128], P(None, 'gx', 'yz'), may hold values from -6 to 6
- direction: float32 [4, 512, 64, 3, 128], P(None, 'gx', 'yz'), may hold values from -6 to 6
- stiffness: float32 [512, 64, 128], P('gx', 'yz'), may hold values from 0.5 to 13.52
- coupling: float32 [512, 64, 128], P('gx', 'yz'), may hold values from 0.5 to 2
- lower_factor: float32 [64, 8, 384, 384], P('gx', 'yz'), may hold values from -0.122474487 to 1
- upper_factor: float32 [64, 8, 384, 384], P('gx', 'yz'), may hold values from -0.122474487 to 2, as said below
- pivot_order: int32 [64, 8, 384], P('gx', 'yz'), may hold values from 0 to 383, each once within a row
- coarse_basis: float32 [4, 512, 64, 128], P(None, 'gx', 'yz'), may hold values from 0.2 to 1
- coarse_inverse: float32 [64, 8, 12, 6144], P('gx', 'yz'), may hold values from -0.00024917498 to 0.009765625
- inner_prior: float32 [4], replicated, may hold values from 6291456 to 25165824
Outputs:
- solution_next: float32 [4, 512, 64, 3, 128], P(None, 'gx', 'yz')
- residual_next: float32 [4, 512, 64, 3, 128], P(None, 'gx', 'yz')
- direction_next: float32 [4, 512, 64, 3, 128], P(None, 'gx', 'yz')
- inner_next: float32 [4], replicated
Inputs may be any that keep to these rules, and one draw needn't show every extreme that they name: `upper_factor`: upper triangular with positive diagonal.
All inputs are finite; a program needn't handle non-finite values.
Results may differ from a plain program's by a relative error of at most 0.000067.
Values sent between devices are 32-bit elements; how exact they have to be, the bound alone decides.
No kernel may reach another device: no remote copies, remote signals or barrier semaphores. Data moves between devices by JAX's collectives and lax.ppermute only.
A program may use at most 64 MiB of HBM per device.

v0:
```python
import jax
import jax.numpy as jnp
from jax import lax
from jax.sharding import PartitionSpec as P

precise = lax.Precision.HIGHEST


def with_halo(cells, sides, width):
    for axis, dim in sides:
        count = lax.axis_size(axis)
        ends = count - 1
        head = lax.slice_in_dim(cells, 0, width, axis=dim)
        tail = lax.slice_in_dim(cells, cells.shape[dim] - width, cells.shape[dim], axis=dim)
        cells = jnp.concatenate(
            [
                lax.ppermute(tail, axis, [(i, (i + 1) % count) for i in range(ends)]),
                cells,
                lax.ppermute(head, axis, [((i + 1) % count, i) for i in range(ends)]),
            ],
            axis=dim,
        )
    return cells


def stencil(padded, scaled):
    zero_plane = jnp.zeros_like(scaled[..., :1])
    upward = jnp.concatenate([scaled[..., 1:], zero_plane], axis=4)
    downward = jnp.concatenate([zero_plane, scaled[..., :-1]], axis=4)
    beside = padded[:, 2:, 1:-1] + padded[:, :-2, 1:-1] + padded[:, 1:-1, 2:] + padded[:, 1:-1, :-2]
    return 6.0 * scaled - beside - upward - downward


def operate(direction, stiffness, coupling):
    scaled = stiffness[None, :, :, None, :] * direction
    padded = with_halo(scaled, (("gx", 1), ("yz", 2)), 1)
    return stiffness[None, :, :, None, :] * stencil(padded, scaled) + coupling[
        None, :, :, None, :
    ] * jnp.sum(direction, axis=3, keepdims=True)


def local_solve(field, lower_factor, upper_factor, pivot_order):
    line_width = lower_factor.shape[-1]
    line_rows = field.reshape(-1, line_width)
    pivots = pivot_order.reshape(line_width)
    inverse_order = jnp.argsort(pivots)
    permuted = jnp.take(line_rows, pivots, axis=1)
    middle = jnp.dot(
        permuted, lower_factor[0, 0].T, precision=precise, preferred_element_type=jnp.float32
    )
    solved = jnp.dot(
        middle, upper_factor[0, 0].T, precision=precise, preferred_element_type=jnp.float32
    )
    return jnp.take(solved, inverse_order, axis=1).reshape(field.shape)


def across(padded, field):
    field_shape = field.shape
    blank_rows = jnp.zeros(field_shape[:1] + (field_shape[1] - 2,) + field_shape[2:], field.dtype)
    across_first = jnp.concatenate([padded[:, :1, 1:-1], blank_rows, padded[:, -1:, 1:-1]], axis=1)
    blank_cols = jnp.zeros(field_shape[:2] + (field_shape[2] - 2,) + field_shape[3:], field.dtype)
    across_second = jnp.concatenate([padded[:, 1:-1, :1], blank_cols, padded[:, 1:-1, -1:]], axis=2)
    return field + 0.5 * (across_first + across_second)


def restrict(coarse_basis, field):
    weighted = jnp.einsum("pxyz,cxykz->ckp", coarse_basis, field, precision=precise)
    return weighted.reshape(field.shape[0], -1)


def prolong(coarse_basis, coarse_values, field_shape):
    shaped = coarse_values.reshape(field_shape[0], field_shape[3], coarse_basis.shape[0])
    return jnp.einsum("pxyz,ckp->cxykz", coarse_basis, shaped, precision=precise)


def per_device(
    solution,
    residual,
    direction,
    stiffness,
    coupling,
    lower_factor,
    upper_factor,
    pivot_order,
    coarse_basis,
    coarse_inverse,
    inner_prior,
):
    case_count = residual.shape[0]
    applied = operate(direction, stiffness, coupling)
    curve_part = jnp.sum(direction * applied, axis=(1, 2, 3, 4))
    curvature = lax.psum(curve_part, ("gx", "yz"))
    step_size = inner_prior / curvature
    step_field = step_size[:, None, None, None, None]
    residual_next = residual - step_field * applied
    primal = restrict(coarse_basis, residual_next)
    primal_all = lax.all_gather(primal[:, None, :], ("gx", "yz"), axis=1, tiled=True).reshape(
        case_count, -1
    )
    coarse_values = jnp.dot(
        primal_all, coarse_inverse[0, 0].T, precision=precise, preferred_element_type=jnp.float32
    )
    correction = prolong(coarse_basis, coarse_values, residual.shape)
    local_part = local_solve(residual_next, lower_factor, upper_factor, pivot_order)
    padded = with_halo(local_part, (("gx", 1), ("yz", 2)), 1)
    smoothed = across(padded, local_part)
    preconditioned = smoothed + correction
    inner_part = jnp.sum(residual_next * preconditioned, axis=(1, 2, 3, 4))
    inner_next = lax.psum(inner_part, ("gx", "yz"))
    growth = (inner_next / inner_prior)[:, None, None, None, None]
    direction_next = preconditioned + growth * direction
    solution_next = solution + step_field * direction
    return (solution_next, residual_next, direction_next, inner_next)


def solution(mesh):
    in_specs = (
        P(None, "gx", "yz", None, None),
        P(None, "gx", "yz", None, None),
        P(None, "gx", "yz", None, None),
        P("gx", "yz", None),
        P("gx", "yz", None),
        P("gx", "yz", None, None),
        P("gx", "yz", None, None),
        P("gx", "yz", None),
        P(None, "gx", "yz", None),
        P("gx", "yz", None, None),
        P(),
    )
    out_specs = (
        P(None, "gx", "yz", None, None),
        P(None, "gx", "yz", None, None),
        P(None, "gx", "yz", None, None),
        P(),
    )
    return jax.shard_map(
        per_device, mesh=mesh, in_specs=in_specs, out_specs=out_specs, check_vma=False
    )
```

profile of v0, /device:TPU:1, one launch (start us, length us, event | category | flops | bytes accessed | tf_op | source)
XLA Modules:
  0.0 2391.1 jit_solution(16158936149588700655)
XLA Ops:
  0.6 0.0 copy-start
  0.6 1.3 copy_multiply_fusion
  2.0 8.7 collective-permute-start
  10.8 0.0 copy-start.10
  10.8 0.0 copy-start.1
  10.8 2.1 collective-permute-start.1
  12.8 0.3 fusion.30
  13.2 3.8 sort.17
  17.1 0.1 copy.50
  17.2 0.7 reduce.1
  17.9 0.1 dot_general.20
  18.0 0.1 pad.6.clone
  18.1 11.2 collective-permute-start.3
  29.3 1.3 collective-permute-start.2
  30.6 3.7 collective-permute-done.3
  34.3 10.0 collective-permute-done.2
  44.3 0.7 multiply_reduce_fusion.1
  45.0 103.4 %psum.14 = f32[4]{0:T(128)S(1)} all-reduce(f32[4]{0:T(128)S(1)} %get-tuple-element.19), channel_id=1, replica_groups=mesh['gx'=64,'yz'=8] {'gx','yz'}, use_global_device_ids=true, to_apply=%region_2.0 | all-reduce | flops 4 | bytes 32 | tf_op jit(solution)/shard_map/psum | solution.py:92
  148.5 0.3 copy_subtract_fusion
  148.8 0.0 copy-start.8
  148.9 0.0 copy-start.2
  148.9 0.8 copy-done.8
  149.7 1.6 convolution_bitcast_fusion.1
  151.3 0.1 broadcast_in_dim_reshape.3
  151.4 0.2 copy.56
  151.6 1.7 gather_fusion
  153.3 1.5 fusion.2
  154.8 0.8 fusion
  155.6 1.7 gather_fusion.1
  157.3 0.1 select_bitcast_fusion
  157.4 0.2 copy.58
  157.6 2.6 collective-permute-start.4
  160.2 2047.1 %all_gather.3 = f32[4,512,12]{2,0,1:T(4,128)S(1)} all-gather(f32[4,1,12]{2,0,1:T(4,128)S(1)} %broadcast_in_dim_reshape.3), channel_id=1, replica_groups=mesh['gx'=64,'yz'=8] {'gx','yz'}, dimensions={1}, use_global_device_ids=true | all-gather | bytes 98496 | tf_op jit(solution)/shard_map/all_gather | solution.py:97
  2207.3 0.1 copy.66
  2207.4 0.7 reshape.66
  2208.1 1.9 collective-permute-start.5
  2210.1 0.3 constant_dynamic-update-slice_fusion.1
  2210.4 15.4 collective-permute-done.5
  2225.8 1.3 collective-permute-start.7
  2227.1 12.9 collective-permute-start.6
  2240.0 3.3 convolution_bitcast_fusion.2
  2243.3 0.0 copy-start.4
  2243.3 1.0 multiply_reduce_fusion
  2244.3 144.2 %psum.15 = f32[4]{0:T(128)S(1)} all-reduce(f32[4]{0:T(128)S(1)} %get-tuple-element.33), channel_id=1, replica_groups=mesh['gx'=64,'yz'=8] {'gx','yz'}, use_global_device_ids=true, to_apply=%region_5.7 | all-reduce | flops 4 | bytes 32 | tf_op jit(solution)/shard_map/psum | solution.py:109
  2388.5 0.5 copy-done.12
  2389.0 0.6 multiply_add_fusion
  2389.6 0.8 copy.69
  2390.4 0.8 copy.71
  (47 shorter events, 0.3 us)
Async XLA Ops:
  0.6 152.6 %copy-start = (f32[1,1,384,384]{3,2,1,0:T(8,128)S(1)}, f32[1,1,384,384]{3,2,1,0:T(8,128)}, u32[]{:S(2)}) copy-start(f32[1,1,384,384]{3,2,1,0:T(8,128)} %param.18) | copy-start | bytes 1769476
  2.0 16.1 collective-permute-start
  10.8 2.4 copy-start.10
  10.8 2.4 copy-start.1
  10.8 7.3 collective-permute-start.1
  13.2 3.8 copy-start.9
  13.2 3.9 copy-start.6
  18.1 26.2 %copy-start.7 = (f32[8,8,128]{2,1,0:T(8,128)S(1)}, f32[8,8,128]{2,1,0:T(8,128)}, u32[]{:S(2)}) copy-start(f32[8,8,128]{2,1,0:T(8,128)} %param.16) | copy-start | bytes 98308
  18.1 16.2 collective-permute-start.3
  29.3 15.0 collective-permute-start.2
  44.3 104.2 %copy-start.5 = (f32[4,8,8,3,128]{4,2,3,1,0:T(8,128)S(1)}, f32[4,8,8,3,128]{4,2,3,1,0:T(8,128)}, u32[]{:S(2)}) copy-start(f32[4,8,8,3,128]{4,2,3,1,0:T(8,128)} %param.14) | copy-start | bytes 1179652
  45.0 103.5 %copy-start.11 = (f32[4]{0:T(128)S(1)}, f32[4]{0:T(128)}, u32[]{:S(2)}) copy-start(f32[4]{0:T(128)} %param.23) | copy-start | bytes 52
  148.8 0.9 copy-start.8
  148.9 2.7 copy-start.2
  153.3 1.5 copy-start.3
  157.6 2052.4 %collective-permute-start.4 = (f32[4,1,8,3,128]{4,0,2,1,3:T(4,128)S(1)}, f32[4,1,8,3,128]{4,0,2,1,3:T(4,128)S(1)}, u32[]{:S(2)}, u32[]{:S(2)}) collective-permute-start(f32[4,1,8,3,128]{4,0,2,1,3:T(4,128)S(1)} %copy.96), channel_id=1, source_target_pairs={{0,8},{8,16},{16,24},{24,32},{32,40},{40,48},{48,56},{56,64},{64,7... | collective-permute-start | bytes 147464 | tf_op jit(solution)/shard_map/ppermute | solution.py:17
  2208.1 17.6 collective-permute-start.5
  2225.8 17.5 collective-permute-start.7
  2227.1 16.2 collective-permute-start.6
  2243.3 145.7 %copy-start.4 = (f32[4,8,8,3,128]{4,2,3,1,0:T(8,128)S(1)}, f32[4,8,8,3,128]{4,2,3,1,0:T(8,128)}, u32[]{:S(2)}) copy-start(f32[4,8,8,3,128]{4,2,3,1,0:T(8,128)} %param.13) | copy-start | bytes 1179652
  2388.5 0.5 copy-start.12
where the time goes:
time: 2390 us
  blocking collectives  2290 us (96%)
  starting transfers between devices  42 us (2%)
  waiting for transfers between devices  29.1 us (1%)
    all_gather x1, blocking collectives, per_device(): lax.all_gather(primal[:, None, :], ('gx', 'yz'), axis=1, tiled=True)  2050 us
    psum x1, blocking collectives, per_device(): inner_next = lax.psum(inner_part, ('gx', 'yz'))  144 us
    psum x1, blocking collectives, per_device(): curvature = lax.psum(curve_part, ('gx', 'yz'))  103 us
  transfers between devices with their start and end apart: 8, of which 3 were waited for; matrix products, arithmetic and copies ran while one was open for 0% of the time, Pallas kernels for 0%

commit v1 on v0

--- a/solution.py
+++ b/solution.py
@@ -106,7 +106,8 @@
     smoothed = across(padded, local_part)
     preconditioned = smoothed + correction
     inner_part = jnp.sum(residual_next * preconditioned, axis=(1, 2, 3, 4))
-    inner_next = lax.psum(inner_part, ("gx", "yz"))
+    parts = lax.all_gather(inner_part, ("gx", "yz"))
+    inner_next = jnp.sum(parts, axis=0)
     growth = (inner_next / inner_prior)[:, None, None, None, None]
     direction_next = preconditioned + growth * direction
     solution_next = solution + step_field * direction

time: 2390 us -> 2390 us (level)
    psum x1 -> x0, blocking collectives: 144 us -> none  [per_device(): inner_next = lax.psum(inner_part, ('gx', 'yz'))]
    unnamed x0 -> x1, blocking collectives: none -> 144 us
where the time goes in v1:
time: 2390 us
  blocking collectives  2290 us (96%)
  starting transfers between devices  42 us (2%)
  waiting for transfers between devices  29.1 us (1%)
    all_gather x1, blocking collectives, per_device(): lax.all_gather(primal[:, None, :], ('gx', 'yz'), axis=1, tiled=True)  2050 us
    unnamed x1, blocking collectives  144 us
    psum x1, blocking collectives, per_device(): curvature = lax.psum(curve_part, ('gx', 'yz'))  103 us
  transfers between devices with their start and end apart: 8, of which 3 were waited for; matrix products, arithmetic and copies ran while one was open for 0% of the time, Pallas kernels for 0%

profile of v1, /device:TPU:1, one launch (start us, length us, event | category | flops | bytes accessed | tf_op | source)
XLA Modules:
  0.0 2391.8 jit_solution(15710393862742560780)
XLA Ops:
  0.6 0.0 copy-start
  0.6 1.3 copy_multiply_fusion
  2.0 8.7 collective-permute-start
  10.8 0.0 copy-start.1
  10.8 2.1 collective-permute-start.1
  12.8 0.3 fusion.30
  13.2 3.8 sort.17
  17.1 0.1 copy.50
  17.2 0.7 reduce.1
  17.9 0.1 dot_general.20
  18.0 0.1 pad.6.clone
  18.1 11.2 collective-permute-start.3
  29.3 1.3 collective-permute-start.2
  30.6 3.7 collective-permute-done.3
  34.3 10.0 collective-permute-done.2
  44.3 0.7 multiply_reduce_fusion.1
  45.0 103.4 %psum.7 = f32[4]{0:T(128)S(1)} all-reduce(f32[4]{0:T(128)S(1)} %get-tuple-element.19), channel_id=1, replica_groups=mesh['gx'=64,'yz'=8] {'gx','yz'}, use_global_device_ids=true, to_apply=%region_2.0 | all-reduce | flops 4 | bytes 32 | tf_op jit(solution)/shard_map/psum | solution.py:92
  148.5 0.3 copy_subtract_fusion
  148.9 0.0 copy-start.2
  148.9 0.8 copy-done.8
  149.7 1.6 convolution_bitcast_fusion.1
  151.3 0.1 broadcast_in_dim_reshape.3
  151.4 0.2 copy.56
  151.6 1.7 gather_fusion
  153.3 1.5 fusion.2
  154.8 0.8 fusion
  155.6 1.7 gather_fusion.1
  157.3 0.1 select_bitcast_fusion
  157.4 0.2 copy.58
  157.6 2.6 collective-permute-start.4
  160.3 2047.0 %all_gather.9 = f32[4,512,12]{2,0,1:T(4,128)S(1)} all-gather(f32[4,1,12]{2,0,1:T(4,128)S(1)} %broadcast_in_dim_reshape.3), channel_id=1, replica_groups=mesh['gx'=64,'yz'=8] {'gx','yz'}, dimensions={1}, use_global_device_ids=true | all-gather | bytes 98496 | tf_op jit(solution)/shard_map/all_gather | solution.py:97
  2207.3 0.1 copy.66
  2207.3 0.7 reshape.69
  2208.1 1.9 collective-permute-start.5
  2210.1 0.3 constant_dynamic-update-slice_fusion.1
  2210.3 15.4 collective-permute-done.5
  2225.8 1.3 collective-permute-start.7
  2227.1 12.9 collective-permute-start.6
  2240.0 3.3 convolution_bitcast_fusion.2
  2243.3 1.0 multiply_reduce_fusion
  2244.3 0.3 dynamic-update-slice
  2244.6 144.2 %all-reduce.2 = f32[2048]{0:T(1024)S(1)} all-reduce(f32[2048]{0:T(1024)S(1)} %dynamic-update-slice), channel_id=2, replica_groups=mesh['gx'=64,'yz'=8] {'gx','yz'}, use_global_device_ids=true, to_apply=%add.2 | all-reduce | flops 2048 | bytes 16384
  2388.8 0.3 reshape.58
  2389.0 0.1 reduce_sum.39
  2389.2 0.5 copy-done.11
  2389.6 0.6 multiply_add_fusion
  2390.2 0.8 copy.69
  2391.0 0.8 copy.71
  (51 shorter events, 0.3 us)
Async XLA Ops:
  0.6 152.7 %copy-start = (f32[1,1,384,384]{3,2,1,0:T(8,128)S(1)}, f32[1,1,384,384]{3,2,1,0:T(8,128)}, u32[]{:S(2)}) copy-start(f32[1,1,384,384]{3,2,1,0:T(8,128)} %param.18) | copy-start | bytes 1769476
  2.0 16.1 collective-permute-start
  10.8 2.4 copy-start.10
  10.8 2.4 copy-start.1
  10.8 7.3 collective-permute-start.1
  13.2 3.8 copy-start.9
  13.2 3.9 copy-start.6
  18.1 26.2 %copy-start.7 = (f32[8,8,128]{2,1,0:T(8,128)S(1)}, f32[8,8,128]{2,1,0:T(8,128)}, u32[]{:S(2)}) copy-start(f32[8,8,128]{2,1,0:T(8,128)} %param.16) | copy-start | bytes 98308
  18.1 16.2 collective-permute-start.3
  29.3 15.0 collective-permute-start.2
  44.3 104.2 %copy-start.5 = (f32[4,8,8,3,128]{4,2,3,1,0:T(8,128)S(1)}, f32[4,8,8,3,128]{4,2,3,1,0:T(8,128)}, u32[]{:S(2)}) copy-start(f32[4,8,8,3,128]{4,2,3,1,0:T(8,128)} %param.14) | copy-start | bytes 1179652
  45.0 103.5 %copy-start.12 = (f32[4]{0:T(128)S(1)}, f32[4]{0:T(128)}, u32[]{:S(2)}) copy-start(f32[4]{0:T(128)} %param.23) | copy-start | bytes 52
  148.8 0.9 copy-start.8
  148.9 2.7 copy-start.2
  153.3 1.5 copy-start.3
  157.6 2052.4 %collective-permute-start.4 = (f32[4,1,8,3,128]{4,0,2,1,3:T(4,128)S(1)}, f32[4,1,8,3,128]{4,0,2,1,3:T(4,128)S(1)}, u32[]{:S(2)}, u32[]{:S(2)}) collective-permute-start(f32[4,1,8,3,128]{4,0,2,1,3:T(4,128)S(1)} %copy.96), channel_id=1, source_target_pairs={{0,8},{8,16},{16,24},{24,32},{32,40},{40,48},{48,56},{56,64},{64,7... | collective-permute-start | bytes 147464 | tf_op jit(solution)/shard_map/ppermute | solution.py:17
  2208.1 17.7 collective-permute-start.5
  2225.8 17.5 collective-permute-start.7
  2227.1 16.2 collective-permute-start.6
  2244.3 145.3 %copy-start.4 = (f32[4,8,8,3,128]{4,2,3,1,0:T(8,128)S(1)}, f32[4,8,8,3,128]{4,2,3,1,0:T(8,128)}, u32[]{:S(2)}) copy-start(f32[4,8,8,3,128]{4,2,3,1,0:T(8,128)} %param.13) | copy-start | bytes 1179652
  2389.1 0.5 copy-start.11
